TPU v7x, 32 devices: a whole 2x2x4 slice. The times are simulated.
32 devices in a mesh: dp: 8 (over z, y), mp: 4 (over x, core).
Axes of the slice: x: 2, y: 2, z: 4, core: 2. Of those that a mesh axis runs over, the one named last changes fastest.
Arguments:
- tokens: bfloat16 [2048, 2048], P('dp'), may hold values from -6 to 6
- out_grad: bfloat16 [2048, 2048], P('dp'), may hold values from -6 to 6
- master: float32 [2368, 3, 7168], P('dp', None, 'mp'), may hold values from -6 to 6
- moment_one: float32 [2368, 3, 7168], P('dp', None, 'mp'), may hold values from -6 to 6
- moment_two: float32 [2368, 3, 7168], P('dp', None, 'mp'), may hold values from 0.05 to 5
- old_offsets: int32 [9], replicated, may hold values from 0 to 2048, as said below
- new_offsets: int32 [9], replicated, may hold values from 0 to 2048, as said below
Outputs:
- new_master: float32 [2880, 3, 7168], P('dp', None, 'mp')
- new_moment_one: float32 [2880, 3, 7168], P('dp', None, 'mp')
- new_moment_two: float32 [2880, 3, 7168], P('dp', None, 'mp')
- layer_output: bfloat16 [2048, 2048], P('dp', 'mp')
Inputs may be any that keep to these rules, and one draw needn't show every extreme that they name: non-decreasing, old_offsets[0] = 0 and old_offsets[8] = 2048; device p holds rows old_offsets[p] to old_offsets[p + 1] - 1 in its first slots; every device holds at least one and at most 296 rows, and some device exactly 296. non-decreasing, new_offsets[0] = 0 and new_offsets[8] = 2048; exactly one device holds no rows, its index at least 2 and at most 3; every other device holds at least one and at most 360 rows, some device exactly 360; a row's device in the new layout is its device in the old layout or the next one along dp.
All inputs are finite; a program needn't handle non-finite values.
Results may differ from a plain program's by a relative error of at most 0.014.
Values may be sent and summed in bfloat16 or wider, within the bound.
A program may use at most 256 MiB of HBM per device.

v0:
```python
import jax
import jax.numpy as jnp
from jax import lax
from jax.sharding import PartitionSpec as P

FEATURE_WIDTH = 2048
FF = 7168


beta_one = 0.9
beta_two = 0.95
learn_rate = 0.01
decay_rate = 0.1
adam_eps = 1e-08
bias_one = 1.0 - 0.9**10
bias_two = 1.0 - 0.95**10


def passed_along(value, axis, by):
    peers = lax.axis_size(axis)
    pairs = [(i, i + by) for i in range(peers) if 0 <= i + by < peers]
    return lax.ppermute(value, axis, pairs)


def lookup(small_table, wanted):
    matches = wanted[..., None] == jnp.arange(small_table.shape[0], dtype=jnp.int32)
    return jnp.sum(jnp.where(matches, small_table, 0), axis=-1)


def row_layout(row_count, capacity, offsets):
    row_index = jnp.arange(row_count, dtype=jnp.int32)
    owner_index = row_index // capacity
    local_index = row_index - owner_index * capacity
    row_start = lookup(offsets, owner_index)
    in_range = local_index < lookup(offsets, owner_index + 1) - row_start
    target = jnp.clip(row_start + local_index, 0, FEATURE_WIDTH - 1)
    return (target, in_range)


def adam_step(master_rows, first_rows, second_rows, grads):
    first_new = beta_one * first_rows + (1.0 - beta_one) * grads
    second_new = beta_two * second_rows + (1.0 - beta_two) * grads * grads
    update = first_new / bias_one / (jnp.sqrt(second_new / bias_two) + adam_eps)
    master_new = master_rows - learn_rate * (update + decay_rate * master_rows)
    return (master_new, first_new, second_new)


def reshard(states, old_offsets, new_offsets, capacity_new):
    capacity_old = states.shape[0]
    from_left = passed_along(states.astype(jnp.bfloat16), "dp", 1).astype(states.dtype)
    device_index = lax.axis_index("dp")
    local_index = jnp.arange(capacity_new, dtype=jnp.int32)
    row_start = lookup(new_offsets, device_index)
    row_count = lookup(new_offsets, device_index + 1) - row_start
    in_range = local_index < row_count
    row_index = jnp.clip(row_start + local_index, 0, FEATURE_WIDTH - 1)
    owner_index = jnp.sum(
        (old_offsets[1:-1][None, :] <= row_index[:, None]).astype(jnp.int32), axis=1
    )
    slot_index = (
        (owner_index - device_index + 1) * capacity_old
        + row_index
        - lookup(old_offsets, owner_index)
    )
    neighbours = jnp.concatenate([from_left, states], axis=0)
    picked = jnp.take(neighbours, slot_index, axis=0, mode="clip")
    return jnp.where(in_range[:, None, None, None], picked, 0.0)


def train_pass(tokens, upstream, weights, layout, capacity, live_flag):
    columns = weights.shape[2]
    scale_in = FEATURE_WIDTH ** (-0.5)
    scale_hidden = FF ** (-0.5)
    contract_rows = (((0,), (0,)), ((), ()))
    shard_piece = lax.all_gather(weights, "dp", axis=0, tiled=True)
    down_rows = jnp.zeros((FEATURE_WIDTH, columns), jnp.bfloat16)
    target, in_range = row_layout(shard_piece.shape[0], capacity, layout)
    shard_piece = jnp.where(in_range[:, None, None], shard_piece, jnp.zeros_like(shard_piece))
    token_columns = jnp.take(tokens, target, axis=1, mode="clip")
    upstream_columns = jnp.take(upstream, target, axis=1, mode="clip")
    gate_sum = jnp.dot(token_columns, shard_piece[:, 0], preferred_element_type=jnp.float32)
    up_sum = jnp.dot(token_columns, shard_piece[:, 1], preferred_element_type=jnp.float32)
    back_sum = jnp.dot(upstream_columns, shard_piece[:, 2], preferred_element_type=jnp.float32)
    placed = jnp.where(in_range, target, FEATURE_WIDTH)
    down_rows = down_rows.at[placed].set(shard_piece[:, 2], mode="drop")
    gate_sum, up_sum, back_sum, down_rows = (gate_sum, up_sum, back_sum, down_rows)
    gate_act = gate_sum * scale_in
    up_act = up_sum * scale_in
    back_grad = back_sum * scale_hidden
    sigmoid_gate = jax.nn.sigmoid(gate_act)
    hidden = (gate_act * sigmoid_gate * up_act).astype(jnp.bfloat16)
    partial_value = (
        lax.dot_general(
            hidden, down_rows, (((1,), (1,)), ((), ())), preferred_element_type=jnp.float32
        )
        * scale_hidden
    )
    partial_value = jnp.where(live_flag, partial_value, 0.0)
    layer_output = lax.psum_scatter(
        partial_value.astype(jnp.bfloat16), "mp", scatter_dimension=1, tiled=True
    )
    gate_grad = (
        back_grad * up_act * sigmoid_gate * (1.0 + gate_act * (1.0 - sigmoid_gate))
    ).astype(jnp.bfloat16)
    up_grad = (back_grad * gate_act * sigmoid_gate).astype(jnp.bfloat16)
    target, in_range = row_layout(lax.axis_size("dp") * capacity, capacity, layout)
    token_columns = jnp.take(tokens, target, axis=1, mode="clip")
    upstream_columns = jnp.take(upstream, target, axis=1, mode="clip")
    gate_part = (
        lax.dot_general(token_columns, gate_grad, contract_rows, preferred_element_type=jnp.float32)
        * scale_in
    )
    up_part = (
        lax.dot_general(token_columns, up_grad, contract_rows, preferred_element_type=jnp.float32)
        * scale_in
    )
    down_part = (
        lax.dot_general(upstream_columns, hidden, contract_rows, preferred_element_type=jnp.float32)
        * scale_hidden
    )
    stacked = jnp.stack([gate_part, up_part, down_part], axis=1)
    grads = lax.psum_scatter(
        jnp.where(in_range[:, None, None], stacked, 0.0).astype(jnp.bfloat16),
        "dp",
        scatter_dimension=0,
        tiled=True,
    ).astype(jnp.float32)
    return (grads, layer_output)


def body(tokens, out_grad, master, moment_one, moment_two, old_offsets, new_offsets):
    devices = lax.axis_size("dp")
    shard_rows = FEATURE_WIDTH // devices
    jitter_rows = shard_rows // (2 * (devices - 1)) + 2
    capacity_new = shard_rows + shard_rows // 4 + 2 * jitter_rows
    device_index = lax.axis_index("dp")
    live_flag = lookup(new_offsets, device_index + 1) != lookup(new_offsets, device_index)
    upstream = jnp.where(live_flag, out_grad, jnp.zeros_like(out_grad))
    states = jnp.stack([master, moment_one, moment_two], axis=1)
    weights = states[:, 0].astype(jnp.bfloat16)
    grads, layer_output = train_pass(
        tokens, upstream, weights, old_offsets, states.shape[0], live_flag
    )
    updated = jnp.stack(adam_step(states[:, 0], states[:, 1], states[:, 2], grads), axis=1)
    updated = reshard(updated, old_offsets, new_offsets, capacity_new)
    return (updated[:, 0], updated[:, 1], updated[:, 2], layer_output)


def solution(mesh):
    placed = (
        P("dp", None),
        P("dp", None),
        P("dp", None, "mp"),
        P("dp", None, "mp"),
        P("dp", None, "mp"),
        P(),
        P(),
    )
    return jax.shard_map(
        body,
        mesh=mesh,
        in_specs=placed,
        out_specs=(P("dp", None, "mp"), P("dp", None, "mp"), P("dp", None, "mp"), P("dp", "mp")),
        check_vma=False,
    )
```

profile of v0, /device:TPU:28, one launch (start us, length us, event | category | flops | bytes accessed | tf_op | source)
XLA Modules:
  0.0 1755.9 jit_solution(16380173346685967132)
XLA Ops:
  7.2 4.9 convert_element_type.30
  15.7 7.7 gather_fusion.1
  23.4 8.1 gather_fusion
  31.6 466.4 %all-gather.2.cloned.1.call-done = bf16[2368,3,1792]{2,0,1:T(8,128)(2,1)} async-done(((bf16[296,3,1792]{2,0,1:T(8,128)(2,1)}), bf16[2368,3,1792]{2,0,1:T(8,128)(2,1)}) %all-gather.2.cloned.1.call-update) | async-done | bytes 25460752 | tf_op jit(solution)/shard_map/all_gather | solution.py:75
  498.0 13.6 broadcast_select_fusion
  524.1 5.7 multiply_bitcast_fusion.1
  529.9 5.9 multiply_bitcast_fusion.2
  535.8 5.9 multiply_bitcast_fusion
  541.7 17.8 %fusion = bf16[2368,3,1792]{2,0,1:T(8,128)(2,1)} fusion(bf16[2368,1,1792]{2,0,1:T(8,128)(2,1)} %multiply_bitcast_fusion, bf16[2368,1,1792]{2,0,1:T(8,128)(2,1)} %multiply_bitcast_fusion.1, bf16[2368,1,1792]{2,0,1:T(8,128)(2,1)} %multiply_bitcast_fusion.2, pred[2368]{0:T(1024)(128)(4,1)S(1)} %fusion.19), kind=kLoop, calls=%fused_computation.5 | loop fusion | flops 89112576 | bytes 50923840 | tf_op jit(solution)/shard_map/convert_element_type | solution.py:123
  561.4 747.0 %all-reduce.3.cloned.1.call-done = bf16[2368,3,1792]{2,0,1:T(8,128)(2,1)} async-done(((bf16[2368,3,1792]{2,0,1:T(8,128)(2,1)}), bf16[2368,3,1792]{2,0,1:T(8,128)(2,1)}) %all-reduce.3.cloned.1.call-update) | async-done | bytes 25460752
  1308.4 11.5 subtract_bitcast_fusion
  1320.0 9.5 maximum_convert_fusion
  1333.7 19.8 %scatter_custom_fusion = bf16[2048,1792]{1,0:T(8,128)(2,1)} fusion(s32[2368]{0:T(1024)S(1)} %get-tuple-element.24, bf16[2368,3,1792]{2,0,1:T(8,128)(2,1)} %copy-done.2, bf16[]{:T(256)} %constant.29.clone.1), kind=kCustom, calls=%fused_computation.23 | custom fusion | bytes 15827456 | tf_op jit(solution)/shard_map/scatter | solution.py:85
  1353.5 6.2 fusion.14
  1359.8 179.2 %collective-permute-done = bf16[296,3,3,1792]{3,0,2,1:T(8,128)(2,1)} collective-permute-done((bf16[296,3,3,1792]{3,0,2,1:T(8,128)(2,1)}, bf16[296,3,3,1792]{3,0,2,1:T(8,128)(2,1)}, u32[]{:S(2)}, u32[]{:S(2)}) %collective-permute-start) | collective-permute-done | bytes 9547808 | tf_op jit(solution)/shard_map/ppermute | solution.py:22
  1538.9 11.7 convert_element_type.37
  1550.6 25.4 %maximum_maximum_fusion = f32[592,3,3,1792]{3,0,2,1:T(8,128)} fusion(f32[296,1,3,1792]{3,0,2,1:T(8,128)} %copy-done.1, f32[296,1,3,1792]{3,0,2,1:T(8,128)} %get-tuple-element.32, f32[296,1,3,1792]{3,0,2,1:T(8,128)} %copy-done, f32[296,3,3,1792]{3,0,2,1:T(8,128)} %convert_element_type.37), kind=kLoop, calls=%fused_computation.6 | loop fusion | flops 28643328 | bytes 76382208 | tf_op jit(solution)/shard_map/concatenate | solution.py:65
  1576.0 66.6 %copy.61 = f32[592,3,3,1792]{3,2,1,0:T(4,128)} copy(f32[592,3,3,1792]{3,0,2,1:T(8,128)} %maximum_maximum_fusion) | data formatting | bytes 76382208 | tf_op jit(solution)/shard_map/concatenate | solution.py:65
  1642.6 50.8 %gather_fusion.2 = f32[360,3,3,1792]{3,2,1,0:T(4,128)} fusion(f32[592,3,3,1792]{3,2,1,0:T(4,128)} %copy.61, s32[1024]{0:T(1024)S(1)} %pad_clamp_fusion.1), kind=kCustom, calls=%fused_computation.2 | custom fusion | bytes 46450080 | tf_op jit(solution)/shard_map/jit(_take)/gather | solution.py:66
  1693.3 21.6 %broadcast_select_fusion.1 = f32[360,3,3,1792]{3,2,1,0:T(4,128)} fusion(f32[360,3,3,1792]{3,2,1,0:T(4,128)} %gather_fusion.2, pred[360]{0:T(512)(128)(4,1)S(1)} %iota_compare_fusion.3), kind=kLoop, calls=%fused_computation.12 | loop fusion | flops 5806080 | bytes 46449000 | tf_op jit(solution)/shard_map/jit(_where)/select_n | solution.py:67
  1714.9 16.4 slice_bitcast_fusion
  1731.4 8.6 copy.64
  1740.0 4.6 copy.63
  1744.6 4.6 copy.62
  (53 shorter events, 18.8 us)
Async XLA Ops:
  7.2 5.1 copy-start.7
  7.2 7.1 copy-start.4
  7.2 7.7 copy-start.5
  7.2 490.8 %all-gather.2.cloned.1.call-start = ((), (), s32[]{:S(2)}) async-start(), calls=%async_computation.1 | async-start | bytes 28643328 | tf_op jit(solution)/shard_map/all_gather | solution.py:75
  12.2 3.2 copy-start.6
  12.2 1296.2 %all-reduce.3.cloned.1.call-start = ((), (), s32[]{:S(2)}) async-start(), calls=%async_computation.3 | async-start | bytes 50921472
  31.6 480.1 %copy-start.3 = (bf16[2368,256]{1,0:T(8,128)(2,1)S(1)}, bf16[2368,256]{1,0:T(8,128)(2,1)}, u32[]{:S(2)}) copy-start(bf16[2368,256]{1,0:T(8,128)(2,1)} %gather_fusion) | copy-start | bytes 3637252
  511.7 8.4 copy-start.2
  524.1 11.6 copy-start.9
  524.1 5.7 copy-start.11
  559.5 0.7 copy-start.8
  559.6 1189.6 %reduce-scatter.3.cloned.1.call-start = ((), (), s32[]{:S(2)}) async-start(), calls=%async_computation.2 | async-start | bytes 1310720 | tf_op jit(solution)/shard_map/reduce_scatter | solution.py:99
  1320.0 9.5 copy-start
  1320.0 9.5 copy-start.1
  1329.5 209.4 %collective-permute-start = (bf16[296,3,3,1792]{3,0,2,1:T(8,128)(2,1)}, bf16[296,3,3,1792]{3,0,2,1:T(8,128)(2,1)}, u32[]{:S(2)}, u32[]{:S(2)}) collective-permute-start(bf16[296,3,3,1792]{3,0,2,1:T(8,128)(2,1)} %maximum_convert_fusion), channel_id=1, source_target_pairs={{0,4},{4,8},{8,12},{12,16},{16,20},{20,24},{24,28},{1,5},{5,9},{9,... | collective-permute-start | bytes 28643336 | tf_op jit(solution)/shard_map/ppermute | solution.py:22
  1333.7 19.8 %copy-start.10 = (bf16[256,1792]{1,0:T(8,128)(2,1)S(1)}, bf16[256,1792]{1,0:T(8,128)(2,1)}, u32[]{:S(2)}) copy-start(bf16[256,1792]{1,0:T(8,128)(2,1)} %copy-done.9) | copy-start | bytes 2752516
Sparse Core Ops, SparseCore 0:
  12.3 485.6 all-gather.1
  559.7 748.7 all-reduce.2
  1359.9 30.4 reduce-scatter.2
where the time goes:
time: 1760 us
  waiting for transfers between devices  1390 us (79%)
  local copies, waits for them, and re-layouts  193 us (11%)
  other arithmetic  119 us (7%)
  matrix products  33 us (2%)
    unnamed x4, waiting for transfers between devices  747 us
    all_gather x1, waiting for transfers between devices, train_pass(): shard_piece = lax.all_gather(weights, 'dp', axis=0, tiled=True)  466 us
    ppermute x1, waiting for transfers between devices, passed_along(): return lax.ppermute(value, axis, pairs)  179 us
    concatenate x1, local copies, waits for them, and re-layouts, reshard(): neighbours = jnp.concatenate([from_left, states], axis=0)  66.6 us
    gather x1, local copies, waits for them, and re-layouts, reshard(): picked = jnp.take(neighbours, slot_index, axis=0, mode='clip')  50.8 us
  transfers between devices with their start and end apart: 4, of which 3 were waited for; matrix products, arithmetic and copies ran while one was open for 15% of the time, Pallas kernels for 0%

commit v1 on v0

--- a/solution.py
+++ b/solution.py
@@ -146,6 +146,132 @@
     return (updated[:, 0], updated[:, 1], updated[:, 2], layer_output)
 
 
+def grown(value, axis, before, after):
+    widths = [(0, 0)] * value.ndim
+    widths[axis] = (before, after)
+    return jnp.pad(value, widths)
+
+
+def token_pass(tokens, upstream, master, old_offsets, new_offsets, capacity_new):
+    peers = lax.axis_size("dp")
+    feature_peers = lax.axis_size("mp")
+    capacity_old, kinds, columns = master.shape
+    width = columns // peers
+    features = tokens.shape[1]
+    scale_in = features ** (-0.5)
+    scale_hidden = (columns * feature_peers) ** (-0.5)
+
+    piece = tokens.shape[0] // feature_peers
+    first_row = lax.axis_index("mp") * piece
+    mine = jnp.stack(
+        [
+            lax.dynamic_slice_in_dim(tokens, first_row, piece, 0),
+            lax.dynamic_slice_in_dim(upstream, first_row, piece, 0),
+        ]
+    )
+    everyone = lax.all_gather(mine, ("dp", "mp"), axis=1, tiled=True)
+    all_tokens, all_upstream = everyone[0], everyone[1]
+
+    weights = master.astype(jnp.bfloat16).transpose(1, 0, 2)
+    weights = weights.reshape(kinds, capacity_old, peers, width).transpose(2, 0, 1, 3)
+    blocks = lax.all_to_all(weights, "dp", 0, 0)
+    rows = jnp.zeros((kinds, features + capacity_old, width), jnp.bfloat16)
+    for peer in range(peers):
+        rows = lax.dynamic_update_slice(rows, blocks[peer], (0, old_offsets[peer], 0))
+    rows = rows[:, :features]
+
+    def product(left, right, left_dim, right_dim):
+        return lax.dot_general(
+            left,
+            right,
+            (((left_dim,), (right_dim,)), ((), ())),
+            preferred_element_type=jnp.float32,
+        )
+
+    gate_act = product(all_tokens, rows[0], 1, 0) * scale_in
+    up_act = product(all_tokens, rows[1], 1, 0) * scale_in
+    back_grad = product(all_upstream, rows[2], 1, 0) * scale_hidden
+    sigmoid_gate = jax.nn.sigmoid(gate_act)
+    hidden = (gate_act * sigmoid_gate * up_act).astype(jnp.bfloat16)
+    gate_grad = (
+        back_grad * up_act * sigmoid_gate * (1.0 + gate_act * (1.0 - sigmoid_gate))
+    ).astype(jnp.bfloat16)
+    up_grad = (back_grad * gate_act * sigmoid_gate).astype(jnp.bfloat16)
+
+    grads = jnp.stack(
+        [
+            (product(all_tokens, gate_grad, 0, 0) * scale_in).astype(jnp.bfloat16),
+            (product(all_tokens, up_grad, 0, 0) * scale_in).astype(jnp.bfloat16),
+            (product(all_upstream, hidden, 0, 0) * scale_hidden).astype(jnp.bfloat16),
+        ]
+    )
+    grads = grown(grads, 1, 0, capacity_new)
+    packed = jnp.stack(
+        [
+            lax.dynamic_slice_in_dim(grads, new_offsets[peer], capacity_new, 1)
+            for peer in range(peers)
+        ]
+    )
+    packed = lax.all_to_all(packed, "dp", 0, 0)
+    grads = packed.transpose(1, 2, 0, 3).reshape(kinds, capacity_new, columns)
+
+    partial_value = (product(hidden, rows[2], 1, 1) * scale_hidden).astype(jnp.bfloat16)
+    partial_value = lax.psum_scatter(partial_value, "mp", scatter_dimension=1, tiled=True)
+    layer_output = lax.psum_scatter(partial_value, "dp", scatter_dimension=0, tiled=True)
+    return grads.astype(jnp.float32), layer_output
+
+
+def token_body(tokens, out_grad, master, moment_one, moment_two, old_offsets, new_offsets):
+    devices = lax.axis_size("dp")
+    capacity_old = master.shape[0]
+    capacity_new = new_capacity(tokens.shape[1], devices)
+    device_index = lax.axis_index("dp")
+    new_start = lookup(new_offsets, device_index)
+    new_end = lookup(new_offsets, device_index + 1)
+    old_start = lookup(old_offsets, device_index)
+    left_start = lookup(old_offsets, jnp.maximum(device_index - 1, 0))
+    live_flag = new_end != new_start
+    upstream = jnp.where(live_flag, out_grad, jnp.zeros_like(out_grad))
+
+    states = [value.transpose(1, 0, 2) for value in (master, moment_one, moment_two)]
+    from_left = [passed_along(value.astype(jnp.bfloat16), "dp", 1) for value in states]
+    grads, layer_output = token_pass(
+        tokens, upstream, master, old_offsets, new_offsets, capacity_new
+    )
+    arrived = jnp.clip(old_start - new_start, 0, capacity_new)
+    left_skip = jnp.clip(new_start - left_start, 0, capacity_old)
+    slot = jnp.arange(capacity_new, dtype=jnp.int32)[None, :, None]
+
+    def placed(own, left):
+        left = lax.dynamic_slice_in_dim(grown(left, 1, 0, capacity_new), left_skip, capacity_new, 1)
+        own = grown(own, 1, capacity_new, capacity_new - capacity_old)
+        own = lax.dynamic_slice_in_dim(own, capacity_new - arrived, capacity_new, 1)
+        return jnp.where(slot < arrived, left.astype(jnp.float32), own)
+
+    rows = [placed(own, left) for own, left in zip(states, from_left)]
+    updated = adam_step(rows[0], rows[1], rows[2], grads)
+    in_range = slot < new_end - new_start
+    updated = [jnp.where(in_range, value, 0.0).transpose(1, 0, 2) for value in updated]
+    layer_output = jnp.where(live_flag, layer_output, jnp.zeros_like(layer_output))
+    return (updated[0], updated[1], updated[2], layer_output)
+
+
+def new_capacity(features, devices):
+    shard_rows = features // devices
+    jitter_rows = shard_rows // (2 * (devices - 1)) + 2
+    return shard_rows + shard_rows // 4 + 2 * jitter_rows
+
+
+def any_body(tokens, out_grad, master, *others):
+    devices = lax.axis_size("dp")
+    columns = master.shape[2]
+    moved_tokens = 3 * tokens.shape[0] * devices
+    moved_rows = 2 * master.shape[1] * columns
+    whole = columns % devices == 0 and tokens.shape[0] % lax.axis_size("mp") == 0
+    chosen = token_body if whole and moved_tokens <= moved_rows else body
+    return chosen(tokens, out_grad, master, *others)
+
+
 def solution(mesh):
     placed = (
         P("dp", None),
@@ -157,7 +283,7 @@
         P(),
     )
     return jax.shard_map(
-        body,
+        any_body,
         mesh=mesh,
         in_specs=placed,
         out_specs=(P("dp", None, "mp"), P("dp", None, "mp"), P("dp", None, "mp"), P("dp", "mp")),

time: 1760 us -> 643 us (0.37)
  waiting for transfers between devices: 1390 us -> 399 us
  local copies, waits for them, and re-layouts: 193 us -> 78.1 us
  other arithmetic: 119 us -> 55.9 us
  between operations: 17.4 us -> 48.6 us
    unnamed x4 -> x3, waiting for transfers between devices: 747 us -> 0.05 us
    all_gather x1, waiting for transfers between devices: 466 us -> 0.01 us  [token_pass(): everyone = lax.all_gather(mine, ('dp', 'mp'), axis=1, tiled=True)]
    all_to_all x0 -> x2, waiting for transfers between devices: none -> 211 us  [the longest x1 128 us: token_pass(): blocks = lax.all_to_all(weights, 'dp', 0, 0)]
    gather x3 -> x0, local copies, waits for them, and re-layouts: 66.6 us -> none  [the longest x1 50.8 us: reshard(): picked = jnp.take(neighbours, slot_index, axis=0, mode='clip')]
    concatenate x1 -> x0, local copies, waits for them, and re-layouts: 66.6 us -> none  [reshard(): neighbours = jnp.concatenate([from_left, states], axis=0)]
    reduce_scatter x1 -> x2, waiting for transfers between devices: 0.01 us -> 49.9 us  [the longest x1 42.9 us: token_pass(): lax.psum_scatter(partial_value, 'dp', scatter_dimension=0, tiled=True)]
    ppermute x1 -> x3, waiting for transfers between devices: 179 us -> 138 us  [passed_along(): return lax.ppermute(value, axis, pairs)]
    transpose x0 -> x2, other arithmetic: none -> 39.9 us  [the longest x1 32.9 us: token_body(): jnp.where(in_range, value, 0.0).transpose(1, 0, 2)]
  transfers between devices with their start and end apart: 4 -> 8, of which waited for: 3 -> 7; matrix products, arithmetic and copies ran while one was open for 15% -> 23% of each run, Pallas kernels for 0% -> 0%
where the time goes in v1:
time: 643 us; the launch traced here: 633 us
  waiting for transfers between devices  399 us (62%)
  local copies, waits for them, and re-layouts  78.1 us (12%)
  other arithmetic  55.9 us (9%)
  between operations  48.6 us (8%)
  matrix products  33.9 us (5%)
  starting transfers between devices  17.4 us (3%)
    ppermute x3, waiting for transfers between devices, passed_along(): return lax.ppermute(value, axis, pairs)  138 us
    all_to_all x1, waiting for transfers between devices, token_pass(): blocks = lax.all_to_all(weights, 'dp', 0, 0)  128 us
    all_to_all x1, waiting for transfers between devices, token_pass(): packed = lax.all_to_all(packed, 'dp', 0, 0)  83.1 us
    reduce_scatter x1, waiting for transfers between devices, token_pass(): lax.psum_scatter(partial_value, 'dp', scatter_dimension=0, tiled=True)  42.9 us
    dynamic_update_slice x8, local copies, waits for them, and re-layouts, token_pass(): lax.dynamic_update_slice(rows, blocks[peer], (0, old_offsets[peer], 0))  36 us
    dot_general x7, matrix products, product(): lax.dot_general(left, right, (((left_dim,), (right_dim,)), ((), ())), pre...  33.9 us
    transpose x1, other arithmetic, token_body(): jnp.where(in_range, value, 0.0).transpose(1, 0, 2)  32.9 us
  transfers between devices with their start and end apart: 8, of which 7 were waited for; matrix products, arithmetic and copies ran while one was open for 23% of the time, Pallas kernels for 0%

profile of v1, /device:TPU:28, one launch (start us, length us, event | category | flops | bytes accessed | tf_op | source)
XLA Modules:
  0.0 633.0 jit_solution(5887110800762922554)
XLA Ops:
  11.8 6.9 %convert_bitcast_fusion.1 = (bf16[3,296,1792]{2,1,0:T(8,128)(2,1)S(1)}, bf16[3,296,1792]{2,1,0:T(8,128)(2,1)}) fusion(f32[296,3,1792]{2,0,1:T(8,128)} %param.9), kind=kLoop, calls=%fused_computation.33 | loop fusion | flops 3182592 | bytes 12730368 | tf_op jit(solution)/shard_map/transpose | solution.py:175
  18.7 6.3 reshape.27
  25.0 4.6 copy.39
  29.7 6.1 all-to-all-start
  51.2 127.6 %all-to-all-done = bf16[8,3,296,224]{3,2,1,0:T(8,128)(2,1)} async-done(((bf16[8,3,296,224]{3,2,1,0:T(8,128)(2,1)}), bf16[8,3,296,224]{3,2,1,0:T(8,128)(2,1)}, u32[]{:S(2)}, u32[]{:S(2)}) %all-to-all-start) | async-done | bytes 3182624 | tf_op jit(solution)/shard_map/all_to_all | solution.py:177
  184.1 4.7 dynamic_update_slice.24
  188.8 4.5 dynamic_update_slice.25
  193.3 4.5 dynamic_update_slice.26
  197.8 4.5 dynamic_update_slice.27
  202.2 4.5 dynamic_update_slice.28
  206.7 4.5 dynamic_update_slice.29
  220.2 6.6 %fusion.19 = f32[2048,224]{0,1:T(8,128)S(1)} fusion(bf16[2,2048,2048]{2,1,0:T(8,128)(2,1)} %all-gather.2.cloned.1.call-done, bf16[3,2344,224]{2,1,0:T(8,128)(2,1)} %dynamic_update_slice.31), kind=kOutput, calls=%fused_computation.35 | convolution fusion | flops 1879506944 | bytes 11272192 | tf_op jit(solution)/shard_map/dot_general | solution.py:184
  233.6 5.9 multiply_convert_fusion
  255.6 5.7 fusion.29
  261.3 7.3 %fusion.22 = f32[2048,224]{0,1:T(8,128)S(1)} fusion(bf16[2,2048,2048]{2,1,0:T(8,128)(2,1)} %all-gather.2.cloned.1.call-done, bf16[3,2344,224]{2,1,0:T(8,128)(2,1)} %dynamic_update_slice.31), kind=kOutput, calls=%fused_computation.38 | convolution fusion | flops 1879506944 | bytes 11272192 | tf_op jit(solution)/shard_map/dot_general | solution.py:184
  282.2 7.1 %all-to-all-start.1 = ((bf16[8,3,360,224]{2,3,1,0:T(8,128)(2,1)}), bf16[8,3,360,224]{2,3,1,0:T(8,128)(2,1)}, u32[]{:S(2)}, u32[]{:S(2)}) async-start(bf16[8,3,360,224]{2,3,1,0:T(8,128)(2,1)} %bitcast_dynamic-update-slice_fusion), calls=%async_computation.1 | async-start | bytes 8257536 | tf_op jit(solution)/shard_map/all_to_all | solution.py:215
  290.9 4.8 bitcast_convert_fusion.1
  304.7 7.0 %reduce-scatter.3.cloned.1.call-done = bf16[2048,512]{1,0:T(8,128)(2,1)} async-done(((bf16[2048,2048]{1,0:T(8,128)(2,1)}), bf16[2048,512]{1,0:T(8,128)(2,1)}) %reduce-scatter.3.cloned.1.call-update) | async-done | bytes 2097168 | tf_op jit(solution)/shard_map/reduce_scatter | solution.py:219
  311.7 83.1 %all-to-all-done.1 = bf16[8,3,360,224]{2,3,1,0:T(8,128)(2,1)} async-done(((bf16[8,3,360,224]{2,3,1,0:T(8,128)(2,1)}), bf16[8,3,360,224]{2,3,1,0:T(8,128)(2,1)}, u32[]{:S(2)}, u32[]{:S(2)}) %all-to-all-start.1) | async-done | bytes 3870752 | tf_op jit(solution)/shard_map/all_to_all | solution.py:215
  401.9 8.7 %copy.41 = f32[3,360,1792]{2,1,0:T(8,128)} copy(f32[3,360,1792]{1,2,0:T(8,128)} %bitcast.126) | data formatting | bytes 15482880 | tf_op jit(solution)/shard_map/convert_element_type | solution.py:221
  412.8 68.2 %collective-permute-done.1 = bf16[3,296,1792]{2,1,0:T(8,128)(2,1)} collective-permute-done((bf16[3,296,1792]{2,1,0:T(8,128)(2,1)}, bf16[3,296,1792]{2,1,0:T(8,128)(2,1)}, u32[]{:S(2)}, u32[]{:S(2)}) %collective-permute-start.1) | collective-permute-done | bytes 3182624 | tf_op jit(solution)/shard_map/ppermute | solution.py:22
  481.0 68.0 %collective-permute-done.2 = bf16[3,296,1792]{2,1,0:T(8,128)(2,1)S(1)} collective-permute-done((bf16[3,296,1792]{2,1,0:T(8,128)(2,1)}, bf16[3,296,1792]{2,1,0:T(8,128)(2,1)S(1)}, u32[]{:S(2)}, u32[]{:S(2)}) %collective-permute-start.2) | collective-permute-done | bytes 3182624 | tf_op jit(solution)/shard_map/ppermute | solution.py:22
  549.0 32.9 %select_bitcast_fusion = (f32[360,3,1792]{2,0,1:T(8,128)}, f32[360,3,1792]{2,0,1:T(8,128)}, f32[360,3,1792]{2,0,1:T(8,128)}) fusion(pred[360]{0:T(512)(128)(4,1)S(1)} %iota_compare_fusion.2, f32[3,360,1792]{2,1,0:T(8,128)} %copy.41, s32[]{:T(128)S(6)} %select_n.113, f32[3,296,1792]{2,1,0:T(8,128)} %bitcast.128, s32[]{:T(128)S(6)} %min.8, ...), kind=kLoop, calls=%fused_computation.15 | loop fusion | flops 61931520 | bytes 59609816 | tf_op jit(solution)/shard_map/transpose | solution.py:254
  581.9 42.9 %reduce-scatter.5.cloned.1.call-done = bf16[256,512]{1,0:T(8,128)(2,1)} async-done(((bf16[2048,512]{1,0:T(8,128)(2,1)}), bf16[256,512]{1,0:T(8,128)(2,1)}) %reduce-scatter.5.cloned.1.call-update) | async-done | bytes 262160 | tf_op jit(solution)/shard_map/reduce_scatter | solution.py:220
  (63 shorter events, 57.6 us)
Async XLA Ops:
  7.2 213.0 %all-gather.2.cloned.1.call-start = ((), (), s32[]{:S(2)}) async-start(), calls=%async_computation.4 | async-start | bytes 17301504 | tf_op jit(solution)/shard_map/all_gather | solution.py:172
  29.6 6.1 copy-start.2
  29.7 149.2 %all-to-all-start = ((bf16[8,3,296,224]{3,2,1,0:T(8,128)(2,1)}), bf16[8,3,296,224]{3,2,1,0:T(8,128)(2,1)}, u32[]{:S(2)}, u32[]{:S(2)}) async-start(bf16[8,3,296,224]{3,2,1,0:T(8,128)(2,1)} %copy.39), calls=%async_computation | async-start | bytes 7274496 | tf_op jit(solution)/shard_map/all_to_all | solution.py:177
  35.8 275.9 %reduce-scatter.3.cloned.1.call-start = ((), (), s32[]{:S(2)}) async-start(), calls=%async_computation.5 | async-start | bytes 10485760 | tf_op jit(solution)/shard_map/reduce_scatter | solution.py:219
  220.2 6.6 %copy-start = (bf16[3,2344,224]{2,1,0:T(8,128)(2,1)S(1)}, bf16[3,2344,224]{2,1,0:T(8,128)(2,1)}, u32[]{:S(2)}) copy-start(bf16[3,2344,224]{2,1,0:T(8,128)(2,1)} %dynamic_update_slice.31) | copy-start | bytes 9451012
  220.2 9.6 %copy-start.3 = (bf16[2,2048,2048]{2,1,0:T(8,128)(2,1)S(1)}, bf16[2,2048,2048]{2,1,0:T(8,128)(2,1)}, u32[]{:S(2)}) copy-start(bf16[2,2048,2048]{2,1,0:T(8,128)(2,1)} %all-gather.2.cloned.1.call-done) | copy-start | bytes 50331652
  239.4 0.7 copy-start.1
  255.6 13.0 %slice-start.2 = ((s8[16777216]{0:T(1024)(128)(4,1)}), s8[4194304]{0:T(1024)(128)(4,1)S(1)}, s32[]{:S(2)}) async-start(s8[16777216]{0:T(1024)(128)(4,1)} %bitcast.133), calls=%async_computation.9 | async-start | bytes 8388608
  255.6 13.0 %slice-start.3 = ((s8[16777216]{0:T(1024)(128)(4,1)}), s8[4194304]{0:T(1024)(128)(4,1)S(1)}, s32[]{:S(2)}) async-start(s8[16777216]{0:T(1024)(128)(4,1)} %bitcast.133), calls=%async_computation.10 | async-start | bytes 8388608
  261.3 7.3 %slice-start.4 = ((s8[16777216]{0:T(1024)(128)(4,1)}), s8[4194304]{0:T(1024)(128)(4,1)S(1)}, s32[]{:S(2)}) async-start(s8[16777216]{0:T(1024)(128)(4,1)} %bitcast.133), calls=%async_computation.11 | async-start | bytes 8388608
  261.3 7.3 %slice-start.5 = ((s8[16777216]{0:T(1024)(128)(4,1)}), s8[4194304]{0:T(1024)(128)(4,1)S(1)}, s32[]{:S(2)}) async-start(s8[16777216]{0:T(1024)(128)(4,1)} %bitcast.133), calls=%async_computation.12 | async-start | bytes 8388608
  268.7 2.2 copy-start.4
  282.2 14.8 %slice-start = ((s8[6365184]{0:T(1024)(128)(4,1)}), s8[2170880]{0:T(1024)(128)(4,1)S(1)}, s32[]{:S(2)}) async-start(s8[6365184]{0:T(1024)(128)(4,1)} %bitcast.129), calls=%async_computation.7 | async-start | bytes 4341760
  282.2 112.7 %all-to-all-start.1 = ((bf16[8,3,360,224]{2,3,1,0:T(8,128)(2,1)}), bf16[8,3,360,224]{2,3,1,0:T(8,128)(2,1)}, u32[]{:S(2)}, u32[]{:S(2)}) async-start(bf16[8,3,360,224]{2,3,1,0:T(8,128)(2,1)} %bitcast_dynamic-update-slice_fusion), calls=%async_computation.1 | async-start | bytes 8257536 | tf_op jit(solution)/shard_map/all_to_all | solution.py:215
  289.3 335.5 %reduce-scatter.5.cloned.1.call-start = ((), (), s32[]{:S(2)}) async-start(), calls=%async_computation.6 | async-start | bytes 2359296 | tf_op jit(solution)/shard_map/reduce_scatter | solution.py:220
  289.3 7.7 %slice-start.1 = ((s8[6365184]{0:T(1024)(128)(4,1)}), s8[4194304]{0:T(1024)(128)(4,1)S(1)}, s32[]{:S(2)}) async-start(s8[6365184]{0:T(1024)(128)(4,1)} %bitcast.129), calls=%async_computation.8 | async-start | bytes 8388608
  289.3 123.5 %collective-permute-start = (bf16[3,296,1792]{2,1,0:T(8,128)(2,1)}, bf16[3,296,1792]{2,1,0:T(8,128)(2,1)}, u32[]{:S(2)}, u32[]{:S(2)}) collective-permute-start(bf16[3,296,1792]{2,1,0:T(8,128)(2,1)} %get-tuple-element.24), channel_id=1, source_target_pairs={{0,4},{4,8},{8,12},{12,16},{16,20},{20,24},{24,28},{1,5},{5,9},{9,... | collective-permute-start | bytes 9547784 | tf_op jit(solution)/shard_map/ppermute | solution.py:22
  295.7 185.3 %collective-permute-start.1 = (bf16[3,296,1792]{2,1,0:T(8,128)(2,1)}, bf16[3,296,1792]{2,1,0:T(8,128)(2,1)}, u32[]{:S(2)}, u32[]{:S(2)}) collective-permute-start(bf16[3,296,1792]{2,1,0:T(8,128)(2,1)} %bitcast_convert_fusion.1), channel_id=1, source_target_pairs={{0,4},{4,8},{8,12},{12,16},{16,20},{20,24},{24,28},{1,5},{5,9},{9,... | collective-permute-start | bytes 9547784 | tf_op jit(solution)/shard_map/ppermute | solution.py:22
  299.0 250.0 %collective-permute-start.2 = (bf16[3,296,1792]{2,1,0:T(8,128)(2,1)}, bf16[3,296,1792]{2,1,0:T(8,128)(2,1)S(1)}, u32[]{:S(2)}, u32[]{:S(2)}) collective-permute-start(bf16[3,296,1792]{2,1,0:T(8,128)(2,1)} %bitcast_convert_fusion), channel_id=1, source_target_pairs={{0,4},{4,8},{8,12},{12,16},{16,20},{20,24},{24,28},{1,5},{5,9},{9,... | collective-permute-start | bytes 9547784 | tf_op jit(solution)/shard_map/ppermute | solution.py:22
Sparse Core Ops, SparseCore 0:
  11.9 173.0 all-gather.1
  239.6 72.0 reduce-scatter.2
  315.2 309.5 reduce-scatter.4

commit v2 on v1

--- a/solution.py
+++ b/solution.py
@@ -2,6 +2,7 @@
 import jax.numpy as jnp
 from jax import lax
 from jax.sharding import PartitionSpec as P
+
 
 FEATURE_WIDTH = 2048
 FF = 7168
@@ -152,11 +153,24 @@
     return jnp.pad(value, widths)
 
 
+def lane_split(columns, peers):
+    return -(-columns // (peers * 128)) * 128
+
+
+def product(left, right, left_dim, right_dim):
+    return lax.dot_general(
+        left,
+        right,
+        (((left_dim,), (right_dim,)), ((), ())),
+        preferred_element_type=jnp.float32,
+    )
+
+
 def token_pass(tokens, upstream, master, old_offsets, new_offsets, capacity_new):
     peers = lax.axis_size("dp")
     feature_peers = lax.axis_size("mp")
     capacity_old, kinds, columns = master.shape
-    width = columns // peers
+    width = lane_split(columns, peers)
     features = tokens.shape[1]
     scale_in = features ** (-0.5)
     scale_hidden = (columns * feature_peers) ** (-0.5)
@@ -172,21 +186,22 @@
     everyone = lax.all_gather(mine, ("dp", "mp"), axis=1, tiled=True)
     all_tokens, all_upstream = everyone[0], everyone[1]
 
-    weights = master.astype(jnp.bfloat16).transpose(1, 0, 2)
-    weights = weights.reshape(kinds, capacity_old, peers, width).transpose(2, 0, 1, 3)
+    weights = master.astype(jnp.bfloat16)
+    flat = [grown(weights[:, kind], 1, 0, peers * width - columns) for kind in range(kinds)]
+    weights = jnp.stack(
+        [
+            jnp.concatenate([value[:, peer * width : (peer + 1) * width] for value in flat], 1)
+            for peer in range(peers)
+        ]
+    )
     blocks = lax.all_to_all(weights, "dp", 0, 0)
-    rows = jnp.zeros((kinds, features + capacity_old, width), jnp.bfloat16)
-    for peer in range(peers):
-        rows = lax.dynamic_update_slice(rows, blocks[peer], (0, old_offsets[peer], 0))
-    rows = rows[:, :features]
-
-    def product(left, right, left_dim, right_dim):
-        return lax.dot_general(
-            left,
-            right,
-            (((left_dim,), (right_dim,)), ((), ())),
-            preferred_element_type=jnp.float32,
-        )
+    blocks = blocks.reshape(peers * capacity_old, kinds * width)
+    target, in_range = row_layout(peers * capacity_old, capacity_old, old_offsets)
+    target = jnp.where(in_range, target, features)
+    wanted = jnp.arange(features, dtype=jnp.int32)[:, None] == target[None, :]
+    rows = product(wanted.astype(jnp.bfloat16), blocks, 1, 0).astype(jnp.bfloat16)
+    rows = lax.optimization_barrier(rows)
+    rows = [rows[:, kind * width : (kind + 1) * width] for kind in range(kinds)]
 
     gate_act = product(all_tokens, rows[0], 1, 0) * scale_in
     up_act = product(all_tokens, rows[1], 1, 0) * scale_in
@@ -198,30 +213,40 @@
     ).astype(jnp.bfloat16)
     up_grad = (back_grad * gate_act * sigmoid_gate).astype(jnp.bfloat16)
 
-    grads = jnp.stack(
+    grads = jnp.concatenate(
         [
             (product(all_tokens, gate_grad, 0, 0) * scale_in).astype(jnp.bfloat16),
             (product(all_tokens, up_grad, 0, 0) * scale_in).astype(jnp.bfloat16),
             (product(all_upstream, hidden, 0, 0) * scale_hidden).astype(jnp.bfloat16),
-        ]
-    )
-    grads = grown(grads, 1, 0, capacity_new)
+        ],
+        axis=1,
+    )
+    grads = grown(grads, 0, 0, capacity_new)
     packed = jnp.stack(
         [
-            lax.dynamic_slice_in_dim(grads, new_offsets[peer], capacity_new, 1)
+            lax.dynamic_slice_in_dim(grads, new_offsets[peer], capacity_new, 0)
             for peer in range(peers)
         ]
     )
     packed = lax.all_to_all(packed, "dp", 0, 0)
-    grads = packed.transpose(1, 2, 0, 3).reshape(kinds, capacity_new, columns)
+    grads = [
+        jnp.concatenate(
+            [packed[peer, :, kind * width : (kind + 1) * width] for peer in range(peers)], 1
+        )[:, :columns]
+        for kind in range(kinds)
+    ]
 
     partial_value = (product(hidden, rows[2], 1, 1) * scale_hidden).astype(jnp.bfloat16)
     partial_value = lax.psum_scatter(partial_value, "mp", scatter_dimension=1, tiled=True)
     layer_output = lax.psum_scatter(partial_value, "dp", scatter_dimension=0, tiled=True)
-    return grads.astype(jnp.float32), layer_output
-
-
-def token_body(tokens, out_grad, master, moment_one, moment_two, old_offsets, new_offsets):
+    return jnp.stack(grads).astype(jnp.float32), layer_output
+
+
+def token_body(*arguments):
+    return token_step(*arguments)
+
+
+def token_step(tokens, out_grad, master, moment_one, moment_two, old_offsets, new_offsets):
     devices = lax.axis_size("dp")
     capacity_old = master.shape[0]
     capacity_new = new_capacity(tokens.shape[1], devices)
@@ -234,7 +259,9 @@
     upstream = jnp.where(live_flag, out_grad, jnp.zeros_like(out_grad))
 
     states = [value.transpose(1, 0, 2) for value in (master, moment_one, moment_two)]
-    from_left = [passed_along(value.astype(jnp.bfloat16), "dp", 1) for value in states]
+    from_left = []
+    for value in states:
+        from_left.append(passed_along(value.astype(jnp.bfloat16), "dp", 1))
     grads, layer_output = token_pass(
         tokens, upstream, master, old_offsets, new_offsets, capacity_new
     )
@@ -267,7 +294,7 @@
     columns = master.shape[2]
     moved_tokens = 3 * tokens.shape[0] * devices
     moved_rows = 2 * master.shape[1] * columns
-    whole = columns % devices == 0 and tokens.shape[0] % lax.axis_size("mp") == 0
+    whole = tokens.shape[0] % lax.axis_size("mp") == 0
     chosen = token_body if whole and moved_tokens <= moved_rows else body
     return chosen(tokens, out_grad, master, *others)
 

time: 643 us -> 626 us (0.974)
  local copies, waits for them, and re-layouts: 78.1 us -> 26.4 us
  waiting for transfers between devices: 399 us -> 427 us
  matrix products: 33.9 us -> 48.2 us
  between operations: 48.6 us -> 34.3 us
  other arithmetic: 55.9 us -> 64 us
    dynamic_update_slice x8 -> x0, local copies, waits for them, and re-layouts: 36 us -> none  [token_pass(): lax.dynamic_update_slice(rows, blocks[peer], (0, old_offsets[peer], 0))]
    all_gather x1, waiting for transfers between devices: 0.01 us -> 26.3 us  [token_pass(): everyone = lax.all_gather(mine, ('dp', 'mp'), axis=1, tiled=True)]
    reduce_scatter x1, waiting for transfers between devices: 42.9 us -> 67.3 us  [token_pass(): lax.psum_scatter(partial_value, 'dp', scatter_dimension=0, tiled=True)]
    all_to_all x1, waiting for transfers between devices: 128 us -> 112 us  [token_pass(): blocks = lax.all_to_all(weights, 'dp', 0, 0)]
    dot_general x7 -> x8, matrix products: 33.9 us -> 48.2 us  [product(): lax.dot_general(left, right, (((left_dim,), (right_dim,)), ((), ())), pre...]
    convert_element_type x2 -> x0, local copies, waits for them, and re-layouts: 12.6 us -> none  [token_pass(): return (grads.astype(jnp.float32), layer_output)]
    unnamed x29 -> x41, local copies, waits for them, and re-layouts: 10.9 us -> 22.3 us
    transpose x2, other arithmetic: 39.9 us -> 31.7 us  [token_step(): jnp.where(in_range, value, 0.0).transpose(1, 0, 2)]
  transfers between devices with their start and end apart: 8 -> 8, of which waited for: 7 -> 7; matrix products, arithmetic and copies ran while one was open for 23% -> 18% of each run, Pallas kernels for 0% -> 0%
where the time goes in v2:
time: 626 us; the launch traced here: 616 us
  waiting for transfers between devices  427 us (68%)
  other arithmetic  64 us (10%)
  matrix products  48.2 us (8%)
  between operations  34.3 us (5%)
  local copies, waits for them, and re-layouts  26.4 us (4%)
  starting transfers between devices  16.4 us (3%)
    ppermute x3, waiting for transfers between devices, passed_along(): return lax.ppermute(value, axis, pairs)  142 us
    all_to_all x1, waiting for transfers between devices, token_pass(): blocks = lax.all_to_all(weights, 'dp', 0, 0)  112 us
    all_to_all x1, waiting for transfers between devices, token_pass(): packed = lax.all_to_all(packed, 'dp', 0, 0)  78.4 us
    reduce_scatter x1, waiting for transfers between devices, token_pass(): lax.psum_scatter(partial_value, 'dp', scatter_dimension=0, tiled=True)  67.3 us
    dot_general x8, matrix products, product(): lax.dot_general(left, right, (((left_dim,), (right_dim,)), ((), ())), pre...  48.2 us
    transpose x2, other arithmetic, token_step(): jnp.where(in_range, value, 0.0).transpose(1, 0, 2)  31.7 us
    all_gather x1, waiting for transfers between devices, token_pass(): everyone = lax.all_gather(mine, ('dp', 'mp'), axis=1, tiled=True)  26.3 us
    unnamed x41, local copies, waits for them, and re-layouts  22.3 us
  transfers between devices with their start and end apart: 8, of which 7 were waited for; matrix products, arithmetic and copies ran while one was open for 18% of the time, Pallas kernels for 0%

profile of v2, /device:TPU:28, one launch (start us, length us, event | category | flops | bytes accessed | tf_op | source)
XLA Modules:
  0.0 615.9 jit_solution(5324945188610045899)
XLA Ops:
  11.8 6.9 %fusion.75 = (bf16[296,3,1792]{2,0,1:T(8,128)(2,1)S(1)}, bf16[3,296,1792]{2,1,0:T(8,128)(2,1)}) fusion(f32[296,3,1792]{2,0,1:T(8,128)} %param.9), kind=kLoop, calls=%fused_computation.161 | loop fusion | flops 3182592 | bytes 12730368 | tf_op jit(solution)/shard_map/convert_element_type | solution.py:189
  25.6 6.1 all-to-all-start
  31.9 112.3 %all-to-all-done = bf16[8,296,768]{2,1,0:T(8,128)(2,1)} async-done(((bf16[8,296,768]{2,1,0:T(8,128)(2,1)}), bf16[8,296,768]{2,1,0:T(8,128)(2,1)}, u32[]{:S(2)}, u32[]{:S(2)}) %all-to-all-start) | async-done | bytes 3637280 | tf_op jit(solution)/shard_map/all_to_all | solution.py:197
  144.2 13.2 %fusion.20 = bf16[2048,768]{1,0:T(8,128)(2,1)S(1)} fusion(bf16[2368,768]{1,0:T(8,128)(2,1)} %bitcast.17, s32[2368]{0:T(1024)S(1)} %clamp_select_fusion), kind=kOutput, calls=%fused_computation.37 | convolution fusion | flops 7455506432 | bytes 6792448 | tf_op jit(solution)/shard_map/dot_general | solution.py:161
  157.5 26.3 %all-gather.2.cloned.1.call-done = bf16[2,2048,2048]{2,1,0:T(8,128)(2,1)} async-done(((bf16[2,64,2048]{2,1,0:T(8,128)(2,1)}), bf16[2,2048,2048]{2,1,0:T(8,128)(2,1)}) %all-gather.2.cloned.1.call-update) | async-done | bytes 16777232 | tf_op jit(solution)/shard_map/all_gather | solution.py:186
  183.8 6.0 fusion.22
  189.8 2.1 copy-done.2
  191.9 4.3 multiply_convert_fusion.1
  197.2 5.6 multiply_convert_fusion
  219.2 6.1 fusion.25
  225.3 6.9 %fusion.27 = bf16[2048,256]{1,0:T(8,128)(2,1)S(1)} fusion(bf16[2048,256]{1,0:T(8,128)(2,1)S(1)} %copy-done.4, bf16[2,2048,2048]{2,1,0:T(8,128)(2,1)} %all-gather.2.cloned.1.call-done), kind=kOutput, calls=%fused_computation.44 | convolution fusion | flops 2148532224 | bytes 10485760 | tf_op jit(solution)/shard_map/dot_general | solution.py:161
  232.3 2.9 fusion.28
  235.3 3.1 fusion.29
  238.4 3.4 fusion.19
  249.3 6.4 %all-to-all-start.1 = ((bf16[8,360,768]{2,1,0:T(8,128)(2,1)}), bf16[8,360,768]{2,1,0:T(8,128)(2,1)}, u32[]{:S(2)}, u32[]{:S(2)}) async-start(bf16[8,360,768]{2,1,0:T(8,128)(2,1)} %bitcast_dynamic-update-slice_fusion), calls=%async_computation.1 | async-start | bytes 8847360 | tf_op jit(solution)/shard_map/all_to_all | solution.py:231
  255.7 4.9 bitcast_convert_fusion.1
  261.9 4.9 bitcast_convert_fusion
  273.9 78.4 %all-to-all-done.1 = bf16[8,360,768]{2,1,0:T(8,128)(2,1)} async-done(((bf16[8,360,768]{2,1,0:T(8,128)(2,1)}), bf16[8,360,768]{2,1,0:T(8,128)(2,1)}, u32[]{:S(2)}, u32[]{:S(2)}) %all-to-all-start.1) | async-done | bytes 4423712 | tf_op jit(solution)/shard_map/all_to_all | solution.py:231
  366.2 6.5 %collective-permute-done.1 = bf16[3,296,1792]{2,1,0:T(8,128)(2,1)S(1)} collective-permute-done((bf16[3,296,1792]{2,1,0:T(8,128)(2,1)}, bf16[3,296,1792]{2,1,0:T(8,128)(2,1)S(1)}, u32[]{:S(2)}, u32[]{:S(2)}) %collective-permute-start.1) | collective-permute-done | bytes 3182624 | tf_op jit(solution)/shard_map/ppermute | solution.py:23
  372.7 9.1 %select_bitcast_fusion.1 = f32[360,3,1792]{2,0,1:T(8,128)} fusion(pred[360]{0:T(512)(128)(4,1)S(1)} %iota_compare_fusion.8, bf16[1,360,1792]{2,1,0:T(8,128)(2,1)} %bitcast.57, bf16[1,360,1792]{2,1,0:T(8,128)(2,1)} %bitcast.49, bf16[1,360,1792]{2,1,0:T(8,128)(2,1)} %bitcast.41, s32[]{:T(128)S(6)} %select_n.126, f32[3,296,1792]{2,1,0:T(8,128)} %bitcast.199, ...), kind=kLoop, calls=%fused_computation.19 | loop fusion | flops 23224320 | bytes 21160664 | tf_op jit(solution)/shard_map/transpose | solution.py:281
  381.8 67.7 %collective-permute-done.2 = bf16[3,296,1792]{2,1,0:T(8,128)(2,1)} collective-permute-done((bf16[3,296,1792]{2,1,0:T(8,128)(2,1)}, bf16[3,296,1792]{2,1,0:T(8,128)(2,1)}, u32[]{:S(2)}, u32[]{:S(2)}) %collective-permute-start.2) | collective-permute-done | bytes 3182624 | tf_op jit(solution)/shard_map/ppermute | solution.py:23
  449.4 68.1 %collective-permute-done = bf16[3,296,1792]{2,1,0:T(8,128)(2,1)} collective-permute-done((bf16[3,296,1792]{2,1,0:T(8,128)(2,1)}, bf16[3,296,1792]{2,1,0:T(8,128)(2,1)}, u32[]{:S(2)}, u32[]{:S(2)}) %collective-permute-start) | collective-permute-done | bytes 3182624 | tf_op jit(solution)/shard_map/ppermute | solution.py:23
  517.6 22.6 %select_bitcast_fusion = (f32[360,3,1792]{2,0,1:T(8,128)}, f32[360,3,1792]{2,0,1:T(8,128)}) fusion(pred[360]{0:T(512)(128)(4,1)S(1)} %iota_compare_fusion.8, bf16[1,360,1792]{2,1,0:T(8,128)(2,1)} %bitcast.57, bf16[1,360,1792]{2,1,0:T(8,128)(2,1)} %bitcast.49, bf16[1,360,1792]{2,1,0:T(8,128)(2,1)} %bitcast.41, s32[]{:T(128)S(6)} %select_n.126, ...), kind=kLoop, calls=%fused_computation.18 | loop fusion | flops 63866880 | bytes 47997656 | tf_op jit(solution)/shard_map/transpose | solution.py:281
  540.2 67.3 %reduce-scatter.5.cloned.1.call-done = bf16[256,512]{1,0:T(8,128)(2,1)} async-done(((bf16[2048,512]{1,0:T(8,128)(2,1)}), bf16[256,512]{1,0:T(8,128)(2,1)}) %reduce-scatter.5.cloned.1.call-update) | async-done | bytes 262160 | tf_op jit(solution)/shard_map/reduce_scatter | solution.py:241
  (77 shorter events, 40.4 us)
Async XLA Ops:
  7.2 176.6 %all-gather.2.cloned.1.call-start = ((), (), s32[]{:S(2)}) async-start(), calls=%async_computation.4 | async-start | bytes 17301504 | tf_op jit(solution)/shard_map/all_gather | solution.py:186
  25.6 6.2 copy-start.1
  25.6 118.6 %all-to-all-start = ((bf16[8,296,768]{2,1,0:T(8,128)(2,1)}), bf16[8,296,768]{2,1,0:T(8,128)(2,1)}, u32[]{:S(2)}, u32[]{:S(2)}) async-start(bf16[8,296,768]{2,1,0:T(8,128)(2,1)} %fusion.43), calls=%async_computation | async-start | bytes 7274496 | tf_op jit(solution)/shard_map/all_to_all | solution.py:197
  31.7 334.4 %reduce-scatter.3.cloned.1.call-start = ((), (), s32[]{:S(2)}) async-start(), calls=%async_computation.5 | async-start | bytes 10485760 | tf_op jit(solution)/shard_map/reduce_scatter | solution.py:240
  183.8 8.2 %copy-start.2 = (bf16[2,2048,2048]{2,1,0:T(8,128)(2,1)S(1)}, bf16[2,2048,2048]{2,1,0:T(8,128)(2,1)}, u32[]{:S(2)}) copy-start(bf16[2,2048,2048]{2,1,0:T(8,128)(2,1)} %all-gather.2.cloned.1.call-done) | copy-start | bytes 50331652
  191.9 4.3 copy-start.5
  196.2 1.0 copy-start.3
  202.9 0.7 copy-start
  219.1 6.1 copy-start.4
  219.1 13.1 %slice-start.2 = ((s8[16777216]{0:T(1024)(128)(4,1)}), s8[4194304]{0:T(1024)(128)(4,1)S(1)}, s32[]{:S(2)}) async-start(s8[16777216]{0:T(1024)(128)(4,1)} %bitcast.205), calls=%async_computation.9 | async-start | bytes 8388608
  219.2 13.1 %slice-start.3 = ((s8[16777216]{0:T(1024)(128)(4,1)}), s8[4194304]{0:T(1024)(128)(4,1)S(1)}, s32[]{:S(2)}) async-start(s8[16777216]{0:T(1024)(128)(4,1)} %bitcast.205), calls=%async_computation.10 | async-start | bytes 8388608
  225.2 7.0 %slice-start.4 = ((s8[16777216]{0:T(1024)(128)(4,1)}), s8[4194304]{0:T(1024)(128)(4,1)S(1)}, s32[]{:S(2)}) async-start(s8[16777216]{0:T(1024)(128)(4,1)} %bitcast.205), calls=%async_computation.11 | async-start | bytes 8388608
  225.3 7.0 %slice-start.5 = ((s8[16777216]{0:T(1024)(128)(4,1)}), s8[4194304]{0:T(1024)(128)(4,1)S(1)}, s32[]{:S(2)}) async-start(s8[16777216]{0:T(1024)(128)(4,1)} %bitcast.205), calls=%async_computation.12 | async-start | bytes 8388608
  225.3 7.1 %copy-start.6 = (f32[2048,256]{1,0:T(8,128)S(1)}, f32[2048,256]{1,0:T(8,128)}, u32[]{:S(2)}) copy-start(f32[2048,256]{1,0:T(8,128)} %copy-done.5) | copy-start | bytes 6291460
  232.3 2.9 copy-start.7
  249.3 103.0 %all-to-all-start.1 = ((bf16[8,360,768]{2,1,0:T(8,128)(2,1)}), bf16[8,360,768]{2,1,0:T(8,128)(2,1)}, u32[]{:S(2)}, u32[]{:S(2)}) async-start(bf16[8,360,768]{2,1,0:T(8,128)(2,1)} %bitcast_dynamic-update-slice_fusion), calls=%async_computation.1 | async-start | bytes 8847360 | tf_op jit(solution)/shard_map/all_to_all | solution.py:231
  255.7 351.8 %reduce-scatter.5.cloned.1.call-start = ((), (), s32[]{:S(2)}) async-start(), calls=%async_computation.6 | async-start | bytes 2359296 | tf_op jit(solution)/shard_map/reduce_scatter | solution.py:241
  260.6 112.1 %collective-permute-start.1 = (bf16[3,296,1792]{2,1,0:T(8,128)(2,1)}, bf16[3,296,1792]{2,1,0:T(8,128)(2,1)S(1)}, u32[]{:S(2)}, u32[]{:S(2)}) collective-permute-start(bf16[3,296,1792]{2,1,0:T(8,128)(2,1)} %bitcast_convert_fusion.1), channel_id=1, source_target_pairs={{0,4},{4,8},{8,12},{12,16},{16,20},{20,24},{24,28},{1,5},{5,9},{9,... | collective-permute-start | bytes 9547784 | tf_op jit(solution)/shard_map/ppermute | solution.py:23
  266.8 182.6 %collective-permute-start.2 = (bf16[3,296,1792]{2,1,0:T(8,128)(2,1)}, bf16[3,296,1792]{2,1,0:T(8,128)(2,1)}, u32[]{:S(2)}, u32[]{:S(2)}) collective-permute-start(bf16[3,296,1792]{2,1,0:T(8,128)(2,1)} %bitcast_convert_fusion), channel_id=1, source_target_pairs={{0,4},{4,8},{8,12},{12,16},{16,20},{20,24},{24,28},{1,5},{5,9},{9,... | collective-permute-start | bytes 9547784 | tf_op jit(solution)/shard_map/ppermute | solution.py:23
  268.1 249.5 %collective-permute-start = (bf16[3,296,1792]{2,1,0:T(8,128)(2,1)}, bf16[3,296,1792]{2,1,0:T(8,128)(2,1)}, u32[]{:S(2)}, u32[]{:S(2)}) collective-permute-start(bf16[3,296,1792]{2,1,0:T(8,128)(2,1)} %get-tuple-element.13), channel_id=1, source_target_pairs={{0,4},{4,8},{8,12},{12,16},{16,20},{20,24},{24,28},{1,5},{5,9},{9,... | collective-permute-start | bytes 9547784 | tf_op jit(solution)/shard_map/ppermute | solution.py:23
  372.7 144.9 %slice-start = ((s8[6365184]{0:T(1024)(128)(4,1)}), s8[4194304]{0:T(1024)(128)(4,1)S(1)}, s32[]{:S(2)}) async-start(s8[6365184]{0:T(1024)(128)(4,1)} %bitcast.200), calls=%async_computation.7 | async-start | bytes 8388608
  372.7 144.9 %slice-start.1 = ((s8[6365184]{0:T(1024)(128)(4,1)}), s8[2170880]{0:T(1024)(128)(4,1)S(1)}, s32[]{:S(2)}) async-start(s8[6365184]{0:T(1024)(128)(4,1)} %bitcast.200), calls=%async_computation.8 | async-start | bytes 4341760
Sparse Core Ops, SparseCore 0:
  12.0 171.7 all-gather.1
  203.0 72.0 reduce-scatter.2
  366.3 241.1 reduce-scatter.4

commit v3 on v2

--- a/solution.py
+++ b/solution.py
@@ -177,14 +177,13 @@
 
     piece = tokens.shape[0] // feature_peers
     first_row = lax.axis_index("mp") * piece
-    mine = jnp.stack(
-        [
-            lax.dynamic_slice_in_dim(tokens, first_row, piece, 0),
-            lax.dynamic_slice_in_dim(upstream, first_row, piece, 0),
-        ]
-    )
-    everyone = lax.all_gather(mine, ("dp", "mp"), axis=1, tiled=True)
-    all_tokens, all_upstream = everyone[0], everyone[1]
+
+    def everyone(value):
+        mine = lax.dynamic_slice_in_dim(value, first_row, piece, 0)
+        return lax.all_gather(mine, ("dp", "mp"), axis=0, tiled=True)
+
+    all_tokens = everyone(tokens)
+    all_upstream = everyone(upstream)
 
     weights = master.astype(jnp.bfloat16)
     flat = [grown(weights[:, kind], 1, 0, peers * width - columns) for kind in range(kinds)]
@@ -221,13 +220,12 @@
         ],
         axis=1,
     )
-    grads = grown(grads, 0, 0, capacity_new)
-    packed = jnp.stack(
-        [
-            lax.dynamic_slice_in_dim(grads, new_offsets[peer], capacity_new, 0)
-            for peer in range(peers)
-        ]
-    )
+    target, in_range = row_layout(peers * capacity_new, capacity_new, new_offsets)
+    target = jnp.where(in_range, target, features)
+    wanted = target[:, None] == jnp.arange(features, dtype=jnp.int32)[None, :]
+    grads = lax.optimization_barrier(grads)
+    packed = product(wanted.astype(jnp.bfloat16), grads, 1, 0).astype(jnp.bfloat16)
+    packed = packed.reshape(peers, capacity_new, kinds * width)
     packed = lax.all_to_all(packed, "dp", 0, 0)
     grads = [
         jnp.concatenate(
@@ -238,7 +236,9 @@
 
     partial_value = (product(hidden, rows[2], 1, 1) * scale_hidden).astype(jnp.bfloat16)
     partial_value = lax.psum_scatter(partial_value, "mp", scatter_dimension=1, tiled=True)
-    layer_output = lax.psum_scatter(partial_value, "dp", scatter_dimension=0, tiled=True)
+    shares = partial_value.reshape(peers, -1, partial_value.shape[1])
+    shares = lax.all_to_all(shares, "dp", 0, 0)
+    layer_output = jnp.sum(shares.astype(jnp.float32), axis=0).astype(jnp.bfloat16)
     return jnp.stack(grads).astype(jnp.float32), layer_output
 
 

time: 626 us -> 622 us (level)
  starting transfers between devices: 16.4 us -> 31.5 us
  between operations: 34.3 us -> 19.2 us
  local copies, waits for them, and re-layouts: 26.4 us -> 18.6 us
  matrix products: 48.2 us -> 55.6 us
  other arithmetic: 64 us -> 56.9 us
  waiting for transfers between devices: 427 us -> 434 us
    reduce_scatter x1 -> x0, waiting for transfers between devices: 67.3 us -> none  [token_pass(): lax.psum_scatter(partial_value, 'dp', scatter_dimension=0, tiled=True)]
    all_to_all x0 -> x1, waiting for transfers between devices: none -> 58.4 us  [token_pass(): shares = lax.all_to_all(shares, 'dp', 0, 0)]
    all_gather x1 -> x2, waiting for transfers between devices: 26.3 us -> 43.9 us  [everyone(): return lax.all_gather(mine, ('dp', 'mp'), axis=0, tiled=True)]
    all_to_all x0 -> x1, starting transfers between devices: none -> 14.2 us  [token_pass(): shares = lax.all_to_all(shares, 'dp', 0, 0)]
    dot_general x8 -> x9, matrix products: 48.2 us -> 55.6 us  [product(): lax.dot_general(left, right, (((left_dim,), (right_dim,)), ((), ())), pre...]
    unnamed x41 -> x38, local copies, waits for them, and re-layouts: 22.3 us -> 15.4 us
  transfers between devices with their start and end apart: 8 -> 9, of which waited for: 7 -> 6; matrix products, arithmetic and copies ran while one was open for 18% -> 20% of each run, Pallas kernels for 0% -> 0%
where the time goes in v3:
time: 622 us; the launch traced here: 615 us
  waiting for transfers between devices  434 us (70%)
  other arithmetic  56.9 us (9%)
  matrix products  55.6 us (9%)
  starting transfers between devices  31.5 us (5%)
  between operations  19.2 us (3%)
  local copies, waits for them, and re-layouts  18.6 us (3%)
    ppermute x3, waiting for transfers between devices, passed_along(): return lax.ppermute(value, axis, pairs)  137 us
    all_to_all x1, waiting for transfers between devices, token_pass(): blocks = lax.all_to_all(weights, 'dp', 0, 0)  113 us
    all_to_all x1, waiting for transfers between devices, token_pass(): packed = lax.all_to_all(packed, 'dp', 0, 0)  81.3 us
    all_to_all x1, waiting for transfers between devices, token_pass(): shares = lax.all_to_all(shares, 'dp', 0, 0)  58.4 us
    dot_general x9, matrix products, product(): lax.dot_general(left, right, (((left_dim,), (right_dim,)), ((), ())), pre...  55.6 us
    all_gather x2, waiting for transfers between devices, everyone(): return lax.all_gather(mine, ('dp', 'mp'), axis=0, tiled=True)  43.9 us
    transpose x2, other arithmetic, token_step(): jnp.where(in_range, value, 0.0).transpose(1, 0, 2)  31 us
    unnamed x38, local copies, waits for them, and re-layouts  15.4 us
  transfers between devices with their start and end apart: 9, of which 6 were waited for; matrix products, arithmetic and copies ran while one was open for 20% of the time, Pallas kernels for 0%

profile of v3, /device:TPU:28, one launch (start us, length us, event | category | flops | bytes accessed | tf_op | source)
XLA Modules:
  0.0 615.4 jit_solution(16010882927437062207)
XLA Ops:
  13.6 7.0 %fusion.63 = (bf16[296,3,1792]{2,0,1:T(8,128)(2,1)S(1)}, bf16[3,296,1792]{2,1,0:T(8,128)(2,1)}) fusion(f32[296,3,1792]{2,0,1:T(8,128)} %param.9), kind=kLoop, calls=%fused_computation.157 | loop fusion | flops 3182592 | bytes 12730368 | tf_op jit(solution)/shard_map/convert_element_type | solution.py:188
  27.4 6.1 all-to-all-start
  33.8 112.6 %all-to-all-done = bf16[8,296,768]{2,1,0:T(8,128)(2,1)} async-done(((bf16[8,296,768]{2,1,0:T(8,128)(2,1)}), bf16[8,296,768]{2,1,0:T(8,128)(2,1)}, u32[]{:S(2)}, u32[]{:S(2)}) %all-to-all-start) | async-done | bytes 3637280 | tf_op jit(solution)/shard_map/all_to_all | solution.py:196
  146.3 12.8 %fusion.12 = bf16[2048,768]{1,0:T(8,128)(2,1)} fusion(bf16[2368,768]{1,0:T(8,128)(2,1)} %bitcast.13, s32[2368]{0:T(1024)S(1)} %clamp_select_fusion), kind=kOutput, calls=%fused_computation.27 | convolution fusion | flops 7455506432 | bytes 6792448 | tf_op jit(solution)/shard_map/dot_general | solution.py:161
  159.2 6.1 convolution_multiply_fusion.3
  166.2 4.1 multiply_convert_fusion.1
  170.3 5.7 multiply_convert_fusion
  176.8 43.9 %all-gather.5.cloned.1.call-done = bf16[2048,2048]{1,0:T(8,128)(2,1)} async-done(((bf16[64,2048]{1,0:T(8,128)(2,1)}), bf16[2048,2048]{1,0:T(8,128)(2,1)}) %all-gather.5.cloned.1.call-update) | async-done | bytes 8388624 | tf_op jit(solution)/shard_map/all_gather | solution.py:183
  220.7 6.2 %convolution_multiply_fusion.5 = f32[2048,256]{1,0:T(8,128)S(1)} fusion(bf16[2048,2048]{1,0:T(8,128)(2,1)} %all-gather.5.cloned.1.call-done, bf16[2048,768]{1,0:T(8,128)(2,1)} %fusion.12), kind=kOutput, calls=%fused_computation.34 | convolution fusion | flops 2148007936 | bytes 11534336 | tf_op jit(solution)/shard_map/dot_general | solution.py:161
  226.9 2.9 fusion.15
  230.7 2.9 fusion.14
  233.6 3.0 fusion.13
  236.9 11.9 %fusion.11 = bf16[2880,768]{1,0:T(8,128)(2,1)} fusion(bf16[2048,768]{1,0:T(8,128)(2,1)S(1)} %pad_maximum_fusion.1, s32[2880]{0:T(1024)S(1)} %clamp_select_fusion.1), kind=kOutput, calls=%fused_computation.25 | convolution fusion | flops 9067806720 | bytes 7580928 | tf_op jit(solution)/shard_map/dot_general | solution.py:161
  248.8 7.2 %all-to-all-start.1 = ((bf16[8,360,768]{2,1,0:T(8,128)(2,1)}), bf16[8,360,768]{2,1,0:T(8,128)(2,1)}, u32[]{:S(2)}, u32[]{:S(2)}) async-start(bf16[8,360,768]{2,1,0:T(8,128)(2,1)} %bitcast.158), calls=%async_computation.1 | async-start | bytes 8847360 | tf_op jit(solution)/shard_map/all_to_all | solution.py:229
  256.0 5.0 bitcast_convert_fusion.1
  271.2 81.3 %all-to-all-done.1 = bf16[8,360,768]{2,1,0:T(8,128)(2,1)} async-done(((bf16[8,360,768]{2,1,0:T(8,128)(2,1)}), bf16[8,360,768]{2,1,0:T(8,128)(2,1)}, u32[]{:S(2)}, u32[]{:S(2)}) %all-to-all-start.1) | async-done | bytes 4423712 | tf_op jit(solution)/shard_map/all_to_all | solution.py:229
  352.5 2.0 fusion.50
  364.4 2.0 fusion.44
  366.4 14.2 %all-to-all-start.2 = ((bf16[8,256,512]{2,1,0:T(8,128)(2,1)}), bf16[8,256,512]{2,1,0:T(8,128)(2,1)S(1)}, u32[]{:S(2)}, u32[]{:S(2)}) async-start(bf16[8,256,512]{2,1,0:T(8,128)(2,1)} %bitcast.159), calls=%async_computation.3 | async-start | bytes 4194304 | tf_op jit(solution)/shard_map/all_to_all | solution.py:240
  380.7 8.1 %select_bitcast_fusion.1 = f32[360,3,1792]{2,0,1:T(8,128)} fusion(pred[360]{0:T(512)(128)(4,1)S(1)} %iota_compare_fusion.13, bf16[1,360,1792]{2,1,0:T(8,128)(2,1)} %bitcast.38, bf16[1,360,1792]{2,1,0:T(8,128)(2,1)} %bitcast.30, bf16[1,360,1792]{2,1,0:T(8,128)(2,1)} %bitcast.22, s32[]{:T(128)S(6)} %select_n.138, f32[3,296,1792]{2,1,0:T(8,128)} %bitcast.150, ...), kind=kLoop, calls=%fused_computation.20 | loop fusion | flops 23224320 | bytes 21160664 | tf_op jit(solution)/shard_map/transpose | solution.py:281
  388.7 69.3 %collective-permute-done.2 = bf16[3,296,1792]{2,1,0:T(8,128)(2,1)} collective-permute-done((bf16[3,296,1792]{2,1,0:T(8,128)(2,1)}, bf16[3,296,1792]{2,1,0:T(8,128)(2,1)}, u32[]{:S(2)}, u32[]{:S(2)}) %collective-permute-start.2) | collective-permute-done | bytes 3182624 | tf_op jit(solution)/shard_map/ppermute | solution.py:23
  458.0 68.2 %collective-permute-done = bf16[3,296,1792]{2,1,0:T(8,128)(2,1)} collective-permute-done((bf16[3,296,1792]{2,1,0:T(8,128)(2,1)}, bf16[3,296,1792]{2,1,0:T(8,128)(2,1)}, u32[]{:S(2)}, u32[]{:S(2)}) %collective-permute-start) | collective-permute-done | bytes 3182624 | tf_op jit(solution)/shard_map/ppermute | solution.py:23
  526.2 22.9 %select_bitcast_fusion = (f32[360,3,1792]{2,0,1:T(8,128)}, f32[360,3,1792]{2,0,1:T(8,128)}) fusion(pred[360]{0:T(512)(128)(4,1)S(1)} %iota_compare_fusion.13, bf16[1,360,1792]{2,1,0:T(8,128)(2,1)} %bitcast.38, bf16[1,360,1792]{2,1,0:T(8,128)(2,1)} %bitcast.30, bf16[1,360,1792]{2,1,0:T(8,128)(2,1)} %bitcast.22, s32[]{:T(128)S(6)} %select_n.138, ...), kind=kLoop, calls=%fused_computation.19 | loop fusion | flops 63866880 | bytes 47997656 | tf_op jit(solution)/shard_map/transpose | solution.py:281
  549.2 58.4 %all-to-all-done.2 = bf16[8,256,512]{2,1,0:T(8,128)(2,1)S(1)} async-done(((bf16[8,256,512]{2,1,0:T(8,128)(2,1)}), bf16[8,256,512]{2,1,0:T(8,128)(2,1)S(1)}, u32[]{:S(2)}, u32[]{:S(2)}) %all-to-all-start.2) | async-done | bytes 2097184 | tf_op jit(solution)/shard_map/all_to_all | solution.py:240
  (80 shorter events, 32.4 us)
Async XLA Ops:
  7.2 1.2 copy-start
  7.2 152.0 %all-gather.3.cloned.1.call-start = ((), (), s32[]{:S(2)}) async-start(), calls=%async_computation.4 | async-start | bytes 8650752 | tf_op jit(solution)/shard_map/all_gather | solution.py:183
  9.1 211.5 %all-gather.5.cloned.1.call-start = ((), (), s32[]{:S(2)}) async-start(), calls=%async_computation.5 | async-start | bytes 8650752 | tf_op jit(solution)/shard_map/all_gather | solution.py:183
  27.4 6.2 copy-start.3
  27.4 118.9 %all-to-all-start = ((bf16[8,296,768]{2,1,0:T(8,128)(2,1)}), bf16[8,296,768]{2,1,0:T(8,128)(2,1)}, u32[]{:S(2)}, u32[]{:S(2)}) async-start(bf16[8,296,768]{2,1,0:T(8,128)(2,1)} %fusion.29), calls=%async_computation | async-start | bytes 7274496 | tf_op jit(solution)/shard_map/all_to_all | solution.py:196
  33.6 332.8 %reduce-scatter.2.cloned.1.call-start = ((), (), s32[]{:S(2)}) async-start(), calls=%async_computation.6 | async-start | bytes 10485760 | tf_op jit(solution)/shard_map/reduce_scatter | solution.py:238
  159.2 6.2 %copy-start.4 = (bf16[2048,2048]{1,0:T(8,128)(2,1)S(1)}, bf16[2048,2048]{1,0:T(8,128)(2,1)}, u32[]{:S(2)}) copy-start(bf16[2048,2048]{1,0:T(8,128)(2,1)} %all-gather.3.cloned.1.call-done) | copy-start | bytes 25165828
  159.2 7.0 %copy-start.6 = (bf16[2048,768]{1,0:T(8,128)(2,1)S(1)}, bf16[2048,768]{1,0:T(8,128)(2,1)}, u32[]{:S(2)}) copy-start(bf16[2048,768]{1,0:T(8,128)(2,1)} %fusion.12) | copy-start | bytes 9437188
  166.2 4.1 copy-start.7
  220.7 6.2 %copy-start.5 = (bf16[2048,2048]{1,0:T(8,128)(2,1)S(1)}, bf16[2048,2048]{1,0:T(8,128)(2,1)}, u32[]{:S(2)}) copy-start(bf16[2048,2048]{1,0:T(8,128)(2,1)} %all-gather.5.cloned.1.call-done) | copy-start | bytes 25165828
  220.7 9.1 %slice-start.4 = ((s8[8388608]{0:T(1024)(128)(4,1)}), s8[4194304]{0:T(1024)(128)(4,1)S(1)}, s32[]{:S(2)}) async-start(s8[8388608]{0:T(1024)(128)(4,1)} %bitcast.160), calls=%async_computation.11 | async-start | bytes 8388608
  226.9 2.9 slice-start.5
  226.9 3.7 copy-start.8
  230.6 2.9 copy-start.9
  248.8 13.5 %slice-start.2 = ((s8[6365184]{0:T(1024)(128)(4,1)}), s8[2170880]{0:T(1024)(128)(4,1)S(1)}, s32[]{:S(2)}) async-start(s8[6365184]{0:T(1024)(128)(4,1)} %bitcast.156), calls=%async_computation.9 | async-start | bytes 4341760
  248.8 103.7 %all-to-all-start.1 = ((bf16[8,360,768]{2,1,0:T(8,128)(2,1)}), bf16[8,360,768]{2,1,0:T(8,128)(2,1)}, u32[]{:S(2)}, u32[]{:S(2)}) async-start(bf16[8,360,768]{2,1,0:T(8,128)(2,1)} %bitcast.158), calls=%async_computation.1 | async-start | bytes 8847360 | tf_op jit(solution)/shard_map/all_to_all | solution.py:229
  256.0 6.3 %slice-start.3 = ((s8[6365184]{0:T(1024)(128)(4,1)}), s8[4194304]{0:T(1024)(128)(4,1)S(1)}, s32[]{:S(2)}) async-start(s8[6365184]{0:T(1024)(128)(4,1)} %bitcast.156), calls=%async_computation.10 | async-start | bytes 8388608
  260.9 119.7 %collective-permute-start.1 = (bf16[3,296,1792]{2,1,0:T(8,128)(2,1)}, bf16[3,296,1792]{2,1,0:T(8,128)(2,1)}, u32[]{:S(2)}, u32[]{:S(2)}) collective-permute-start(bf16[3,296,1792]{2,1,0:T(8,128)(2,1)} %bitcast_convert_fusion.1), channel_id=1, source_target_pairs={{0,4},{4,8},{8,12},{12,16},{16,20},{20,24},{24,28},{1,5},{5,9},{9,... | collective-permute-start | bytes 9547784 | tf_op jit(solution)/shard_map/ppermute | solution.py:23
  264.2 193.8 %collective-permute-start.2 = (bf16[3,296,1792]{2,1,0:T(8,128)(2,1)}, bf16[3,296,1792]{2,1,0:T(8,128)(2,1)}, u32[]{:S(2)}, u32[]{:S(2)}) collective-permute-start(bf16[3,296,1792]{2,1,0:T(8,128)(2,1)} %bitcast_convert_fusion), channel_id=1, source_target_pairs={{0,4},{4,8},{8,12},{12,16},{16,20},{20,24},{24,28},{1,5},{5,9},{9,... | collective-permute-start | bytes 9547784 | tf_op jit(solution)/shard_map/ppermute | solution.py:23
  265.5 260.7 %collective-permute-start = (bf16[3,296,1792]{2,1,0:T(8,128)(2,1)}, bf16[3,296,1792]{2,1,0:T(8,128)(2,1)}, u32[]{:S(2)}, u32[]{:S(2)}) collective-permute-start(bf16[3,296,1792]{2,1,0:T(8,128)(2,1)} %get-tuple-element.15), channel_id=1, source_target_pairs={{0,4},{4,8},{8,12},{12,16},{16,20},{20,24},{24,28},{1,5},{5,9},{9,... | collective-permute-start | bytes 9547784 | tf_op jit(solution)/shard_map/ppermute | solution.py:23
  366.4 241.1 %all-to-all-start.2 = ((bf16[8,256,512]{2,1,0:T(8,128)(2,1)}), bf16[8,256,512]{2,1,0:T(8,128)(2,1)S(1)}, u32[]{:S(2)}, u32[]{:S(2)}) async-start(bf16[8,256,512]{2,1,0:T(8,128)(2,1)} %bitcast.159), calls=%async_computation.3 | async-start | bytes 4194304 | tf_op jit(solution)/shard_map/all_to_all | solution.py:240
  380.6 145.6 %slice-start = ((s8[6365184]{0:T(1024)(128)(4,1)}), s8[4194304]{0:T(1024)(128)(4,1)S(1)}, s32[]{:S(2)}) async-start(s8[6365184]{0:T(1024)(128)(4,1)} %bitcast.151), calls=%async_computation.7 | async-start | bytes 8388608
  380.7 145.6 %slice-start.1 = ((s8[6365184]{0:T(1024)(128)(4,1)}), s8[2170880]{0:T(1024)(128)(4,1)S(1)}, s32[]{:S(2)}) async-start(s8[6365184]{0:T(1024)(128)(4,1)} %bitcast.151), calls=%async_computation.8 | async-start | bytes 4341760
  526.2 82.4 %copy-start.1 = (bf16[256,2048]{1,0:T(8,128)(2,1)S(1)}, bf16[256,2048]{1,0:T(8,128)(2,1)}, u32[]{:S(2)}) copy-start(bf16[256,2048]{1,0:T(8,128)(2,1)} %param.7) | copy-start | bytes 3145732
  (1 other events, 0.7 us)
Sparse Core Ops, SparseCore 0:
  11.4 129.1 all-gather.2
  144.0 76.5 all-gather.4
  223.2 71.2 reduce-scatter.1
